TPU v7x, 128 devices: a whole 4x4x4 slice. The times are simulated.
128 devices in a mesh: row: 8 (over y, core), col: 16 (over x, z).
Axes of the slice: x: 4, y: 4, z: 4, core: 2. Of those that a mesh axis runs over, the one named last changes fastest.
Arguments:
- tokens: bfloat16 [2048, 8192], P('col', 'row'), may hold values from -6 to 6
- gate_weight: bfloat16 [8192, 28672], P('row', 'col'), may hold values from -0.109375 to 0.109375
- up_weight: bfloat16 [8192, 28672], P('row', 'col'), may hold values from -0.109375 to 0.109375
- down_weight: bfloat16 [28672, 8192], P('col', 'row'), may hold values from -0.0546875 to 0.0546875
- gate_keep: int32 [224, 48], P('col'), may hold values from 0 to 63, as said below
- gate_count: int32 [224], P('col'), may hold values from 5 to 48, as said below
- up_keep: int32 [224, 48], P('col'), may hold values from 0 to 63, as said below
- up_count: int32 [224], P('col'), may hold values from 5 to 48, as said below
- down_keep: int32 [64, 176], P('row'), may hold values from 0 to 223, as said below
- down_count: int32 [64], P('row'), may hold values from 15 to 176, as said below
Outputs:
- output_rows: bfloat16 [2048, 8192], P('col', 'row')
Inputs may be any that keep to these rules, and one draw needn't show every extreme that they name: `gate_keep`: each row holds distinct block indices of the model features. `gate_count`: some block column uses all 48 slots. `up_keep`: each row holds distinct block indices of the model features. `up_count`: some block column uses all 48 slots. `down_keep`: each row holds distinct block indices of the hidden units. `down_count`: some block column uses all 176 slots.
All inputs are finite; a program needn't handle non-finite values.
Results may differ from a plain program's by a relative error of at most 0.028.
Values may be sent and summed in bfloat16 or wider, within the bound.
A program may use at most 128 MiB of HBM per device.

v0:
```python
import jax
import jax.numpy as jnp
from jax import lax
from jax.sharding import PartitionSpec as P

BLOCK = 128


def local_mask(keep_list, keep_count, offset, blocks):
    position = jnp.arange(keep_list.shape[1], dtype=jnp.int32)
    active_slot = position[None, :] < keep_count[:, None]
    local_index = keep_list - offset
    matches = (
        local_index[:, :, None] == jnp.arange(blocks, dtype=jnp.int32)[None, None, :]
    ) & active_slot[:, :, None]
    return jnp.any(matches, axis=1)


def apply_mask(weight, block_mask, block_size):
    block_rows, block_cols = block_mask.shape
    shaped = weight.reshape(block_rows, block_size, block_cols, block_size)
    masked = jnp.where(block_mask[:, None, :, None], shaped, jnp.zeros((), weight.dtype))
    return masked.reshape(weight.shape)


def on_device(
    tokens,
    gate_weight,
    up_weight,
    down_weight,
    gate_keep,
    gate_count,
    up_keep,
    up_count,
    down_keep,
    down_count,
):
    model_blocks = gate_weight.shape[0] // BLOCK
    hidden_blocks = gate_weight.shape[1] // BLOCK
    row_offset = lax.axis_index("row") * model_blocks
    col_offset = lax.axis_index("col") * hidden_blocks
    gate_pruned = apply_mask(
        gate_weight, local_mask(gate_keep, gate_count, row_offset, model_blocks).T, BLOCK
    )
    up_pruned = apply_mask(
        up_weight, local_mask(up_keep, up_count, row_offset, model_blocks).T, BLOCK
    )
    down_pruned = apply_mask(
        down_weight, local_mask(down_keep, down_count, col_offset, hidden_blocks).T, BLOCK
    )
    both_weights = jnp.concatenate([gate_pruned, up_pruned], axis=1)
    hidden_width = gate_weight.shape[1]
    partial_value = jnp.dot(
        lax.all_gather(tokens, "col", axis=0, tiled=True),
        both_weights,
        preferred_element_type=jnp.float32,
    )
    summed = lax.psum(partial_value.astype(jnp.bfloat16), "row").astype(jnp.float32)
    hidden = (jax.nn.silu(summed[:, :hidden_width]) * summed[:, hidden_width:]).astype(jnp.bfloat16)
    return lax.psum_scatter(
        jnp.dot(hidden, down_pruned, preferred_element_type=jnp.float32).astype(jnp.bfloat16),
        "col",
        scatter_dimension=0,
        tiled=True,
    )


def solution(mesh):
    return jax.shard_map(
        on_device,
        mesh=mesh,
        in_specs=(
            P("col", "row"),
            P("row", "col"),
            P("row", "col"),
            P("col", "row"),
            P("col", None),
            P("col"),
            P("col", None),
            P("col"),
            P("row", None),
            P("row"),
        ),
        out_specs=P("col", "row"),
        check_vma=False,
    )
```

profile of v0, /device:TPU:0, one launch (start us, length us, event | category | flops | bytes accessed | tf_op | source)
XLA Modules:
  0.0 369.0 jit_solution(6870458090966092904)
XLA Ops:
  6.5 0.0 all-gather.2.cloned.1.call-start
  6.5 0.7 all-gather.2.cloned.1.call-update
  7.3 0.0 all-reduce.2.cloned.1.call-start
  7.3 6.0 %copy.14 = bf16[1024,1792]{0,1:T(8,128)(2,1)} copy(bf16[1024,1792]{1,0:T(8,128)(2,1)} %param.12) | data formatting | bytes 7340032 | tf_op args[2]
  13.3 0.0 copy-start.4
  13.3 0.0 copy-start.2
  13.3 0.0 copy-start.3
  13.3 0.0 copy-start.5
  13.4 6.0 %copy.13 = bf16[1024,1792]{0,1:T(8,128)(2,1)} copy(bf16[1024,1792]{1,0:T(8,128)(2,1)} %param.11) | data formatting | bytes 7340032 | tf_op args[1]
  19.3 0.0 copy-done.4
  19.3 0.1 iota_compare_fusion.4
  19.4 0.0 copy-done.2
  19.4 0.0 copy-done.3
  19.4 0.3 fusion.16
  19.8 0.0 copy-done.5
  19.8 0.1 iota_compare_fusion.5
  19.8 0.3 fusion.14
  20.2 0.5 broadcast_in_dim.57
  20.7 0.0 copy-start
  20.7 5.1 %bitcast_select_fusion.1 = bf16[1024,1792]{0,1:T(8,128)(2,1)} fusion(bf16[1024,1792]{0,1:T(8,128)(2,1)} %copy.14, pred[224,8,8,128]{3,2,1,0:T(8,128)(4,1)S(1)} %bitcast.23), kind=kLoop, calls=%fused_computation.8 | loop fusion | flops 1835008 | bytes 9175040 | tf_op jit(solution)/shard_map/jit(_where)/select_n | solution.py:22
  25.9 0.5 broadcast_in_dim.54
  26.4 0.0 copy-done
  26.4 2.8 bitcast_select_fusion.2
  29.3 34.3 %all-gather.2.cloned.1.call-done = bf16[2048,1024]{1,0:T(8,128)(2,1)} async-done(((bf16[128,1024]{1,0:T(8,128)(2,1)}), bf16[2048,1024]{1,0:T(8,128)(2,1)}) %all-gather.2.cloned.1.call-update) | async-done | bytes 4194320 | tf_op jit(solution)/shard_map/all_gather | solution.py:54
  63.6 22.4 %fusion.1 = bf16[2048,3584]{0,1:T(8,128)(2,1)} fusion(bf16[2048,1024]{1,0:T(8,128)(2,1)} %all-gather.2.cloned.1.call-done, bf16[1024,1792]{0,1:T(8,128)(2,1)} %bitcast_select_fusion.1, bf16[1024,1792]{0,1:T(8,128)(2,1)} %bitcast_select_fusion.2), kind=kOutput, calls=%fused_computation.3 | convolution fusion | flops 15054405632 | bytes 26214400 | tf_op jit(solution)/shard_map/dot_general | solution.py:53
  86.0 0.0 copy-start.6
  86.0 0.0 copy-start.1
  86.0 0.0 all-reduce.2.cloned.1.call-update
  86.0 0.2 reduce-scatter.2.cloned.1.call-start
  86.3 0.4 copy-done.6
  86.7 0.1 iota_compare_fusion.3
  86.7 0.0 copy-done.1
  86.7 0.3 fusion.12
  87.1 162.2 %all-reduce.2.cloned.1.call-done = bf16[2048,3584]{0,1:T(8,128)(2,1)} async-done(((bf16[2048,3584]{0,1:T(8,128)(2,1)}), bf16[2048,3584]{0,1:T(8,128)(2,1)}) %all-reduce.2.cloned.1.call-update) | async-done | bytes 14680080 | tf_op jit(solution)/shard_map/psum | solution.py:58
  249.3 16.5 %convert_element_type.17 = f32[2048,3584]{0,1:T(8,128)} convert(bf16[2048,3584]{0,1:T(8,128)(2,1)} %all-reduce.2.cloned.1.call-done) | non-fusion elementwise | flops 7340032 | bytes 44040192 | tf_op jit(solution)/shard_map/convert_element_type | solution.py:58
  265.8 0.5 broadcast_in_dim.59
  266.3 17.2 %fusion.7 = bf16[2048,1024]{1,0:T(8,128)(2,1)} fusion(f32[2048,3584]{0,1:T(8,128)} %convert_element_type.17, bf16[1792,1024]{1,0:T(8,128)(2,1)} %param.13, pred[224,8,8,128]{3,2,1,0:T(8,128)(4,1)S(1)} %bitcast.25), kind=kOutput, calls=%fused_computation.11 | convolution fusion | flops 7542145024 | bytes 39059456 | tf_op jit(solution)/shard_map/dot_general | solution.py:61
  283.5 0.0 reduce-scatter.2.cloned.1.call-update
  283.6 78.8 %reduce-scatter.2.cloned.1.call-done = bf16[128,1024]{1,0:T(8,128)(2,1)} async-done(((bf16[2048,1024]{1,0:T(8,128)(2,1)}), bf16[128,1024]{1,0:T(8,128)(2,1)}) %reduce-scatter.2.cloned.1.call-update) | async-done | bytes 262160 | tf_op jit(solution)/shard_map/reduce_scatter | solution.py:60
  (2 shorter events, 0.0 us)
Async XLA Ops:
  6.5 57.0 %all-gather.2.cloned.1.call-start = ((), (), s32[]{:S(2)}) async-start(), calls=%async_computation.1 | async-start | bytes 4456448 | tf_op jit(solution)/shard_map/all_gather | solution.py:54
  7.3 242.0 %all-reduce.2.cloned.1.call-start = ((), (), s32[]{:S(2)}) async-start(), calls=%async_computation.2 | async-start | bytes 29360128 | tf_op jit(solution)/shard_map/psum | solution.py:58
  13.3 6.0 %copy-start.4 = (s32[14]{0:T(128)S(1)}, s32[14]{0:T(128)}, u32[]{:S(2)}) copy-start(s32[14]{0:T(128)} %param.17) | copy-start | bytes 172
  13.3 6.1 %copy-start.2 = (s32[14,48]{1,0:T(8,128)S(1)}, s32[14,48]{1,0:T(8,128)}, u32[]{:S(2)}) copy-start(s32[14,48]{1,0:T(8,128)} %param.16) | copy-start | bytes 8068
  13.3 6.1 %copy-start.3 = (s32[14,48]{1,0:T(8,128)S(1)}, s32[14,48]{1,0:T(8,128)}, u32[]{:S(2)}) copy-start(s32[14,48]{1,0:T(8,128)} %param.14) | copy-start | bytes 8068
  13.3 6.4 %copy-start.5 = (s32[14]{0:T(128)S(1)}, s32[14]{0:T(128)}, u32[]{:S(2)}) copy-start(s32[14]{0:T(128)} %param.15) | copy-start | bytes 172
  20.7 5.7 %copy-start = (bf16[1024,1792]{0,1:T(8,128)(2,1)S(1)}, bf16[1024,1792]{0,1:T(8,128)(2,1)}, u32[]{:S(2)}) copy-start(bf16[1024,1792]{0,1:T(8,128)(2,1)} %copy.13) | copy-start | bytes 11010052
  86.0 0.7 copy-start.6
  86.0 0.7 copy-start.1
  86.0 276.4 %reduce-scatter.2.cloned.1.call-start = ((), (), s32[]{:S(2)}) async-start(), calls=%async_computation.3 | async-start | bytes 4456448 | tf_op jit(solution)/shard_map/reduce_scatter | solution.py:60
Sparse Core Ops, SparseCore 0:
  9.5 54.0 all-gather.1
  86.1 163.0 all-reduce.1
  283.7 78.6 reduce-scatter.1
where the time goes:
time: 369 us
  waiting for transfers between devices  276 us (75%)
  matrix products  39.6 us (11%)
  other arithmetic  25.7 us (7%)
  local copies, waits for them, and re-layouts  14.1 us (4%)
  between operations  13.2 us (4%)
    psum x1, waiting for transfers between devices, on_device(): lax.psum(partial_value.astype(jnp.bfloat16), 'row').astype(jnp.float32)  162 us
    reduce_scatter x1, waiting for transfers between devices, on_device(): lax.psum_scatter(jnp.dot(hidden, down_pruned, preferred_element_type=jnp....  78.8 us
    all_gather x1, waiting for transfers between devices, on_device(): lax.all_gather(tokens, 'col', axis=0, tiled=True)  34.3 us
    dot_general x1, matrix products, on_device(): jnp.dot(lax.all_gather(tokens, 'col', axis=0, tiled=True), both_weights,...  22.4 us
    dot_general x1, matrix products, on_device(): jnp.dot(hidden, down_pruned, preferred_element_type=jnp.float32)  17.2 us
    convert_element_type x1, other arithmetic, on_device(): lax.psum(partial_value.astype(jnp.bfloat16), 'row').astype(jnp.float32)  16.5 us
    unnamed x16, local copies, waits for them, and re-layouts  12.4 us
    select_n x2, other arithmetic, apply_mask(): jnp.where(block_mask[:, None, :, None], shaped, jnp.zeros((), weight.dtype))  7.95 us
  transfers between devices with their start and end apart: 3, of which 3 were waited for; matrix products, arithmetic and copies ran while one was open for 6% of the time, Pallas kernels for 0%

commit v1 on v0

--- a/solution.py
+++ b/solution.py
@@ -4,6 +4,8 @@
 from jax.sharding import PartitionSpec as P
 
 BLOCK = 128
+CHUNKS = 2
+COL_A2A = True
 
 
 def local_mask(keep_list, keep_count, offset, blocks):
@@ -37,6 +39,7 @@
 ):
     model_blocks = gate_weight.shape[0] // BLOCK
     hidden_blocks = gate_weight.shape[1] // BLOCK
+    n_col = lax.axis_size("col")
     row_offset = lax.axis_index("row") * model_blocks
     col_offset = lax.axis_index("col") * hidden_blocks
     gate_pruned = apply_mask(
@@ -50,19 +53,28 @@
     )
     both_weights = jnp.concatenate([gate_pruned, up_pruned], axis=1)
     hidden_width = gate_weight.shape[1]
-    partial_value = jnp.dot(
-        lax.all_gather(tokens, "col", axis=0, tiled=True),
-        both_weights,
-        preferred_element_type=jnp.float32,
-    )
-    summed = lax.psum(partial_value.astype(jnp.bfloat16), "row").astype(jnp.float32)
-    hidden = (jax.nn.silu(summed[:, :hidden_width]) * summed[:, hidden_width:]).astype(jnp.bfloat16)
-    return lax.psum_scatter(
-        jnp.dot(hidden, down_pruned, preferred_element_type=jnp.float32).astype(jnp.bfloat16),
-        "col",
-        scatter_dimension=0,
-        tiled=True,
-    )
+    rows = tokens.shape[0] // CHUNKS
+    outs = []
+    for k in range(CHUNKS):
+        chunk = lax.all_gather(tokens[k * rows:(k + 1) * rows], "col", axis=0, tiled=True)
+        partial_value = jnp.dot(chunk, both_weights, preferred_element_type=jnp.float32)
+        summed = lax.psum_scatter(
+            partial_value.astype(jnp.bfloat16), "row", scatter_dimension=0, tiled=True
+        ).astype(jnp.float32)
+        hidden = (
+            jax.nn.silu(summed[:, :hidden_width]) * summed[:, hidden_width:]
+        ).astype(jnp.bfloat16)
+        hidden = lax.all_gather(hidden, "row", axis=0, tiled=True)
+        terms = jnp.dot(hidden, down_pruned, preferred_element_type=jnp.float32).astype(
+            jnp.bfloat16
+        )
+        if COL_A2A:
+            terms = terms.reshape(n_col, rows, terms.shape[1])
+            terms = lax.all_to_all(terms, "col", 0, 0, tiled=False)
+            outs.append(jnp.sum(terms.astype(jnp.float32), axis=0).astype(jnp.bfloat16))
+        else:
+            outs.append(lax.psum_scatter(terms, "col", scatter_dimension=0, tiled=True))
+    return jnp.concatenate(outs, axis=0)
 
 
 def solution(mesh):

time: 369 us -> 330 us (0.89)
  waiting for transfers between devices: 276 us -> 205 us
  local copies, waits for them, and re-layouts: 14.1 us -> 38.5 us
  starting transfers between devices: 0.26 us -> 11.9 us
  other arithmetic: 25.7 us -> 14.4 us
  matrix products: 39.6 us -> 45.2 us
    psum x1 -> x0, waiting for transfers between devices: 162 us -> none  [on_device(): lax.psum(partial_value.astype(jnp.bfloat16), 'row').astype(jnp.float32)]
    reduce_scatter x1 -> x0, waiting for transfers between devices: 78.8 us -> none  [on_device(): lax.psum_scatter(jnp.dot(hidden, down_pruned, preferred_element_type=jnp....]
    unnamed x3 -> x8, waiting for transfers between devices: 0.74 us -> 73 us
    all_gather x1 -> x4, waiting for transfers between devices: 34.3 us -> 99.3 us  [the longest x2 50.3 us: on_device(): hidden = lax.all_gather(hidden, 'row', axis=0, tiled=True)]
    all_to_all x0 -> x2, waiting for transfers between devices: none -> 32.8 us  [on_device(): terms = lax.all_to_all(terms, 'col', 0, 0, tiled=False)]
    unnamed x16 -> x22, local copies, waits for them, and re-layouts: 12.4 us -> 35.2 us
    convert_element_type x1 -> x4, other arithmetic: 16.5 us -> 2.29 us  [the longest x2 2.05 us: on_device(): hidden = (jax.nn.silu(summed[:, :hidden_width]) * summed[:, hidden_width:...]
    all_to_all x0 -> x2, starting transfers between devices: none -> 11.5 us  [on_device(): terms = lax.all_to_all(terms, 'col', 0, 0, tiled=False)]
  transfers between devices with their start and end apart: 3 -> 8, of which waited for: 3 -> 8; matrix products, arithmetic and copies ran while one was open for 6% -> 29% of each run, Pallas kernels for 0% -> 0%
where the time goes in v1:
time: 330 us; the launch traced here: 329 us
  waiting for transfers between devices  205 us (62%)
  matrix products  45.2 us (14%)
  local copies, waits for them, and re-layouts  38.5 us (12%)
  other arithmetic  14.4 us (4%)
  between operations  13.6 us (4%)
  starting transfers between devices  11.9 us (4%)
    unnamed x8, waiting for transfers between devices  73 us
    all_gather x2, waiting for transfers between devices, on_device(): hidden = lax.all_gather(hidden, 'row', axis=0, tiled=True)  50.3 us
    all_gather x2, waiting for transfers between devices, on_device(): lax.all_gather(tokens[k * rows:(k + 1) * rows], 'col', axis=0, tiled=True)  49 us
    unnamed x22, local copies, waits for them, and re-layouts  35.2 us
    all_to_all x2, waiting for transfers between devices, on_device(): terms = lax.all_to_all(terms, 'col', 0, 0, tiled=False)  32.8 us
    dot_general x2, matrix products, on_device(): jnp.dot(chunk, both_weights, preferred_element_type=jnp.float32)  26.8 us
    dot_general x2, matrix products, on_device(): jnp.dot(hidden, down_pruned, preferred_element_type=jnp.float32)  18.4 us
    all_to_all x2, starting transfers between devices, on_device(): terms = lax.all_to_all(terms, 'col', 0, 0, tiled=False)  11.5 us
  transfers between devices with their start and end apart: 8, of which 8 were waited for; matrix products, arithmetic and copies ran while one was open for 29% of the time, Pallas kernels for 0%

profile of v1, /device:TPU:0, one launch (start us, length us, event | category | flops | bytes accessed | tf_op | source)
XLA Modules:
  0.0 328.8 jit_solution(4209620873377738050)
XLA Ops:
  6.5 0.0 all-gather.5.cloned.1.call-start
  6.5 1.7 fusion.16
  8.2 0.0 all-gather.5.cloned.1.call-update
  8.2 0.0 all-gather.9.cloned.1.call-start
  8.3 0.7 all-gather.9.cloned.1.call-update
  9.0 0.0 reduce-scatter.7.cloned.1.call-start
  9.1 6.0 %copy.16 = bf16[1024,1792]{0,1:T(8,128)(2,1)} copy(bf16[1024,1792]{1,0:T(8,128)(2,1)} %param.12) | data formatting | bytes 7340032 | tf_op args[2]
  15.0 0.0 copy-start.3
  15.0 6.0 %copy.15 = bf16[1024,1792]{0,1:T(8,128)(2,1)} copy(bf16[1024,1792]{1,0:T(8,128)(2,1)} %param.11) | data formatting | bytes 7340032 | tf_op args[1]
  21.0 0.0 copy-done.3
  21.1 0.0 copy-done.4
  21.1 0.0 copy-done.5
  21.1 0.1 iota_compare_fusion.4
  21.1 0.3 fusion.11
  21.5 0.0 copy-done.6
  21.5 0.1 iota_compare_fusion.5
  21.5 0.3 fusion.9
  21.9 0.5 broadcast_in_dim.57
  22.4 0.0 copy-start
  22.4 5.0 %bitcast_select_fusion.1 = bf16[1024,1792]{0,1:T(8,128)(2,1)} fusion(bf16[1024,1792]{0,1:T(8,128)(2,1)} %copy.16, pred[224,8,8,128]{3,2,1,0:T(8,128)(4,1)S(1)} %bitcast.33), kind=kLoop, calls=%fused_computation.4 | loop fusion | flops 1835008 | bytes 9175040 | tf_op jit(solution)/shard_map/jit(_where)/select_n | solution.py:24
  27.4 0.5 broadcast_in_dim.54
  28.0 0.0 copy-done
  28.0 2.8 bitcast_select_fusion.2
  30.8 26.2 %all-gather.5.cloned.1.call-done = bf16[1024,1024]{1,0:T(8,128)(2,1)} async-done(((bf16[64,1024]{1,0:T(8,128)(2,1)}), bf16[1024,1024]{1,0:T(8,128)(2,1)}) %all-gather.5.cloned.1.call-update) | async-done | bytes 2097168 | tf_op jit(solution)/shard_map/all_gather | solution.py:59
  57.0 13.4 %fusion = bf16[1024,3584]{0,1:T(8,128)(2,1)} fusion(bf16[1024,1024]{1,0:T(8,128)(2,1)} %all-gather.5.cloned.1.call-done, bf16[1024,1792]{0,1:T(8,128)(2,1)} %bitcast_select_fusion.1, bf16[1024,1792]{0,1:T(8,128)(2,1)} %bitcast_select_fusion.2), kind=kOutput, calls=%fused_computation.6 | convolution fusion | flops 7534542848 | bytes 16777216 | tf_op jit(solution)/shard_map/dot_general | solution.py:60
  70.4 10.0 %copy.17 = bf16[1024,3584]{1,0:T(8,128)(2,1)} copy(bf16[1024,3584]{0,1:T(8,128)(2,1)} %fusion) | data formatting | bytes 14680064
  80.5 0.0 reduce-scatter.7.cloned.1.call-update
  80.5 0.2 reduce-scatter.9.cloned.1.call-start
  80.7 22.8 %all-gather.9.cloned.1.call-done = bf16[1024,1024]{1,0:T(8,128)(2,1)} async-done(((bf16[64,1024]{1,0:T(8,128)(2,1)}), bf16[1024,1024]{1,0:T(8,128)(2,1)}) %all-gather.9.cloned.1.call-update) | async-done | bytes 2097168 | tf_op jit(solution)/shard_map/all_gather | solution.py:59
  103.5 13.4 %fusion.1 = bf16[1024,3584]{0,1:T(8,128)(2,1)} fusion(bf16[1024,1024]{1,0:T(8,128)(2,1)} %all-gather.9.cloned.1.call-done, bf16[1024,1792]{0,1:T(8,128)(2,1)} %bitcast_select_fusion.1, bf16[1024,1792]{0,1:T(8,128)(2,1)} %bitcast_select_fusion.2), kind=kOutput, calls=%fused_computation.7 | convolution fusion | flops 7534542848 | bytes 16777216 | tf_op jit(solution)/shard_map/dot_general | solution.py:60
  116.9 10.1 %copy.19 = bf16[1024,3584]{1,0:T(8,128)(2,1)} copy(bf16[1024,3584]{0,1:T(8,128)(2,1)} %fusion.1) | data formatting | bytes 14680064
  127.0 0.0 reduce-scatter.9.cloned.1.call-update
  127.0 0.0 all-gather.7.cloned.1.call-start
  127.1 25.6 %reduce-scatter.7.cloned.1.call-done = bf16[128,3584]{1,0:T(8,128)(2,1)} async-done(((bf16[1024,3584]{1,0:T(8,128)(2,1)}), bf16[128,3584]{1,0:T(8,128)(2,1)}) %reduce-scatter.7.cloned.1.call-update) | async-done | bytes 917520
  152.7 1.5 copy.18
  154.2 0.1 convert_element_type.36
  154.4 1.0 fusion.5
  155.4 0.0 all-gather.7.cloned.1.call-update
  155.4 0.0 copy-start.7
  155.4 0.0 copy-start.2
  155.4 0.0 all-gather.11.cloned.1.call-start
  155.5 46.6 %reduce-scatter.9.cloned.1.call-done = bf16[128,3584]{1,0:T(8,128)(2,1)} async-done(((bf16[1024,3584]{1,0:T(8,128)(2,1)}), bf16[128,3584]{1,0:T(8,128)(2,1)}) %reduce-scatter.9.cloned.1.call-update) | async-done | bytes 917520
  202.1 1.5 copy.20
  203.6 0.1 convert_element_type.41
  203.8 1.0 fusion.4
  204.8 0.0 all-gather.11.cloned.1.call-update
  204.8 0.0 copy-done.7
  204.8 0.1 iota_compare_fusion.3
  204.9 0.0 copy-done.2
  204.9 0.3 fusion.7
  205.2 31.3 %all-gather.7.cloned.1.call-done = bf16[1024,1792]{0,1:T(8,128)(2,1)} async-done(((bf16[128,1792]{0,1:T(8,128)(2,1)}), bf16[1024,1792]{0,1:T(8,128)(2,1)}) %all-gather.7.cloned.1.call-update) | async-done | bytes 3670032 | tf_op jit(solution)/shard_map/all_gather | solution.py:67
  236.6 0.5 broadcast_in_dim.59
  237.1 0.0 copy-start.1
  237.1 9.3 %convolution_convert_fusion.3 = bf16[1024,1024]{1,0:T(8,128)(2,1)} fusion(bf16[1024,1792]{0,1:T(8,128)(2,1)} %all-gather.7.cloned.1.call-done, bf16[1792,1024]{1,0:T(8,128)(2,1)} %param.13, pred[224,8,8,128]{3,2,1,0:T(8,128)(4,1)S(1)} %bitcast.37), kind=kOutput, calls=%fused_computation.9 | convolution fusion | flops 3760979968 | bytes 11272192 | tf_op jit(solution)/shard_map/dot_general | solution.py:68
  246.4 0.0 copy-done.1
  246.4 7.0 %all-to-all-start = ((bf16[16,64,1024]{2,1,0:T(8,128)(2,1)}), bf16[16,64,1024]{2,1,0:T(8,128)(2,1)S(1)}, u32[]{:S(2)}, u32[]{:S(2)}) async-start(bf16[16,64,1024]{2,1,0:T(8,128)(2,1)} %bitcast.36), calls=%async_computation | async-start | bytes 4194304 | tf_op jit(solution)/shard_map/all_to_all | solution.py:73
  253.4 19.0 %all-gather.11.cloned.1.call-done = bf16[1024,1792]{0,1:T(8,128)(2,1)} async-done(((bf16[128,1792]{0,1:T(8,128)(2,1)}), bf16[1024,1792]{0,1:T(8,128)(2,1)}) %all-gather.11.cloned.1.call-update) | async-done | bytes 3670032 | tf_op jit(solution)/shard_map/all_gather | solution.py:67
  272.4 9.1 %convolution_convert_fusion.2 = bf16[1024,1024]{1,0:T(8,128)(2,1)} fusion(bf16[1024,1792]{0,1:T(8,128)(2,1)} %all-gather.11.cloned.1.call-done, bf16[1792,1024]{1,0:T(8,128)(2,1)} %param.13, pred[224,8,8,128]{3,2,1,0:T(8,128)(4,1)} %bitcast.38), kind=kOutput, calls=%fused_computation.8 | convolution fusion | flops 3760979968 | bytes 11272192 | tf_op jit(solution)/shard_map/dot_general | solution.py:68
  281.4 2.9 all-to-all-done
  284.3 4.6 %all-to-all-start.1 = ((bf16[16,64,1024]{2,1,0:T(8,128)(2,1)}), bf16[16,64,1024]{2,1,0:T(8,128)(2,1)}, u32[]{:S(2)}, u32[]{:S(2)}) async-start(bf16[16,64,1024]{2,1,0:T(8,128)(2,1)} %bitcast.35), calls=%async_computation.1 | async-start | bytes 4194304 | tf_op jit(solution)/shard_map/all_to_all | solution.py:73
  288.9 0.4 reduce_sum.24
  289.3 29.9 %all-to-all-done.1 = bf16[16,64,1024]{2,1,0:T(8,128)(2,1)} async-done(((bf16[16,64,1024]{2,1,0:T(8,128)(2,1)}), bf16[16,64,1024]{2,1,0:T(8,128)(2,1)}, u32[]{:S(2)}, u32[]{:S(2)}) %all-to-all-start.1) | async-done | bytes 2097184 | tf_op jit(solution)/shard_map/all_to_all | solution.py:73
  319.3 2.0 reduce_sum.25
  321.3 0.7 pad_maximum_fusion.3
  (5 shorter events, 0.0 us)
Async XLA Ops:
  6.5 50.5 %all-gather.5.cloned.1.call-start = ((), (), s32[]{:S(2)}) async-start(), calls=%async_computation.4 | async-start | bytes 2228224 | tf_op jit(solution)/shard_map/all_gather | solution.py:59
  8.2 95.2 %all-gather.9.cloned.1.call-start = ((), (), s32[]{:S(2)}) async-start(), calls=%async_computation.6 | async-start | bytes 2228224 | tf_op jit(solution)/shard_map/all_gather | solution.py:59
  9.0 143.7 %reduce-scatter.7.cloned.1.call-start = ((), (), s32[]{:S(2)}) async-start(), calls=%async_computation.8 | async-start | bytes 8257536
  15.0 6.0 %copy-start.3 = (s32[14,48]{1,0:T(8,128)S(1)}, s32[14,48]{1,0:T(8,128)}, u32[]{:S(2)}) copy-start(s32[14,48]{1,0:T(8,128)} %param.16) | copy-start | bytes 8068
  15.0 6.0 %copy-start.4 = (s32[14,48]{1,0:T(8,128)S(1)}, s32[14,48]{1,0:T(8,128)}, u32[]{:S(2)}) copy-start(s32[14,48]{1,0:T(8,128)} %param.14) | copy-start | bytes 8068
  15.0 6.0 %copy-start.5 = (s32[14]{0:T(128)S(1)}, s32[14]{0:T(128)}, u32[]{:S(2)}) copy-start(s32[14]{0:T(128)} %param.17) | copy-start | bytes 172
  15.0 6.4 %copy-start.6 = (s32[14]{0:T(128)S(1)}, s32[14]{0:T(128)}, u32[]{:S(2)}) copy-start(s32[14]{0:T(128)} %param.15) | copy-start | bytes 172
  22.4 5.5 %copy-start = (bf16[1024,1792]{0,1:T(8,128)(2,1)S(1)}, bf16[1024,1792]{0,1:T(8,128)(2,1)}, u32[]{:S(2)}) copy-start(bf16[1024,1792]{0,1:T(8,128)(2,1)} %copy.15) | copy-start | bytes 11010052
  80.5 121.6 %reduce-scatter.9.cloned.1.call-start = ((), (), s32[]{:S(2)}) async-start(), calls=%async_computation.9 | async-start | bytes 8257536
  127.0 109.5 %all-gather.7.cloned.1.call-start = ((), (), s32[]{:S(2)}) async-start(), calls=%async_computation.5 | async-start | bytes 4128768 | tf_op jit(solution)/shard_map/all_gather | solution.py:67
  155.4 49.4 %copy-start.7 = (s32[8]{0:T(128)S(1)}, s32[8]{0:T(128)}, u32[]{:S(2)}) copy-start(s32[8]{0:T(128)} %param.19) | copy-start | bytes 100
  155.4 49.5 %copy-start.2 = (s32[8,176]{1,0:T(8,128)S(1)}, s32[8,176]{1,0:T(8,128)}, u32[]{:S(2)}) copy-start(s32[8,176]{1,0:T(8,128)} %param.18) | copy-start | bytes 16900
  155.4 116.9 %all-gather.11.cloned.1.call-start = ((), (), s32[]{:S(2)}) async-start(), calls=%async_computation.7 | async-start | bytes 4128768 | tf_op jit(solution)/shard_map/all_gather | solution.py:67
  237.1 9.3 %copy-start.1 = (pred[14,128,8,128]{3,2,1,0:T(8,128)(4,1)}, pred[14,128,8,128]{3,2,1,0:T(8,128)(4,1)S(1)}, u32[]{:S(2)}) copy-start(pred[14,128,8,128]{3,2,1,0:T(8,128)(4,1)S(1)} %broadcast_in_dim.59) | copy-start | bytes 5505028
  246.4 37.9 %all-to-all-start = ((bf16[16,64,1024]{2,1,0:T(8,128)(2,1)}), bf16[16,64,1024]{2,1,0:T(8,128)(2,1)S(1)}, u32[]{:S(2)}, u32[]{:S(2)}) async-start(bf16[16,64,1024]{2,1,0:T(8,128)(2,1)} %bitcast.36), calls=%async_computation | async-start | bytes 4194304 | tf_op jit(solution)/shard_map/all_to_all | solution.py:73
  284.3 34.9 %all-to-all-start.1 = ((bf16[16,64,1024]{2,1,0:T(8,128)(2,1)}), bf16[16,64,1024]{2,1,0:T(8,128)(2,1)}, u32[]{:S(2)}, u32[]{:S(2)}) async-start(bf16[16,64,1024]{2,1,0:T(8,128)(2,1)} %bitcast.35), calls=%async_computation.1 | async-start | bytes 4194304 | tf_op jit(solution)/shard_map/all_to_all | solution.py:73
Sparse Core Ops, SparseCore 0:
  9.5 47.5 all-gather.4
  59.2 44.2 all-gather.8
  105.9 46.7 reduce-scatter.6
  155.0 47.0 reduce-scatter.8
  203.6 32.9 all-gather.6
  238.1 34.2 all-gather.10

commit v2 on v1

--- a/solution.py
+++ b/solution.py
@@ -4,7 +4,7 @@
 from jax.sharding import PartitionSpec as P
 
 BLOCK = 128
-CHUNKS = 2
+CHUNKS = 1
 COL_A2A = True
 
 
@@ -25,6 +25,61 @@
     return masked.reshape(weight.shape)
 
 
+def row_perm(n_row, step):
+    n_y = n_row // 2
+    return [(y * 2 + c, ((y + step) % n_y) * 2 + c) for y in range(n_y) for c in range(2)]
+
+
+def row_reduce_scatter(value, n_row):
+    n_y = n_row // 2
+    r = lax.axis_index("row")
+    y = r // 2
+    core = r % 2
+    rows, width = value.shape
+    halves = value.reshape(2, rows // 2, width)
+    keep = lax.dynamic_index_in_dim(halves, core, 0, keepdims=False)
+    send = lax.dynamic_index_in_dim(halves, 1 - core, 0, keepdims=False)
+    swap = [(i, i ^ 1) for i in range(n_row)]
+    pair = keep.astype(jnp.float32) + lax.ppermute(send, "row", swap).astype(jnp.float32)
+    chunk = rows // 2 // n_y
+    pair = pair.reshape(n_y, chunk, width)
+    results = []
+    for direction, cols in ((1, slice(0, width // 2)), (-1, slice(width // 2, width))):
+        own = pair[:, :, cols]
+        index = (y - direction) % n_y
+        acc = lax.dynamic_index_in_dim(own, index, 0, keepdims=False)
+        for step in range(n_y - 1):
+            got = lax.ppermute(acc.astype(jnp.bfloat16), "row", row_perm(n_row, direction))
+            index = (index - direction) % n_y
+            acc = got.astype(jnp.float32) + lax.dynamic_index_in_dim(own, index, 0, keepdims=False)
+        results.append(acc)
+    return results
+
+
+def row_all_gather(value, n_row):
+    n_y = n_row // 2
+    r = lax.axis_index("row")
+    y = r // 2
+    core = r % 2
+    chunk, width = value.shape
+    parts = []
+    for direction, cols in ((1, slice(0, width // 2)), (-1, slice(width // 2, width))):
+        held = value[:, cols]
+        full = jnp.zeros((n_y, chunk, width // 2), value.dtype)
+        full = lax.dynamic_update_index_in_dim(full, held, y, 0)
+        for step in range(n_y - 1):
+            held = lax.ppermute(held, "row", row_perm(n_row, direction))
+            full = lax.dynamic_update_index_in_dim(full, held, (y - direction * (step + 1)) % n_y, 0)
+        parts.append(full)
+    half = jnp.concatenate(parts, axis=2).reshape(n_y * chunk, width)
+    swap = [(i, i ^ 1) for i in range(n_row)]
+    other = lax.ppermute(half, "row", swap)
+    both = jnp.zeros((2, n_y * chunk, width), value.dtype)
+    both = lax.dynamic_update_index_in_dim(both, half, core, 0)
+    both = lax.dynamic_update_index_in_dim(both, other, 1 - core, 0)
+    return both.reshape(2 * n_y * chunk, width)
+
+
 def on_device(
     tokens,
     gate_weight,
@@ -40,6 +95,7 @@
     model_blocks = gate_weight.shape[0] // BLOCK
     hidden_blocks = gate_weight.shape[1] // BLOCK
     n_col = lax.axis_size("col")
+    n_row = lax.axis_size("row")
     row_offset = lax.axis_index("row") * model_blocks
     col_offset = lax.axis_index("col") * hidden_blocks
     gate_pruned = apply_mask(
@@ -52,19 +108,14 @@
         down_weight, local_mask(down_keep, down_count, col_offset, hidden_blocks).T, BLOCK
     )
     both_weights = jnp.concatenate([gate_pruned, up_pruned], axis=1)
-    hidden_width = gate_weight.shape[1]
     rows = tokens.shape[0] // CHUNKS
     outs = []
     for k in range(CHUNKS):
         chunk = lax.all_gather(tokens[k * rows:(k + 1) * rows], "col", axis=0, tiled=True)
         partial_value = jnp.dot(chunk, both_weights, preferred_element_type=jnp.float32)
-        summed = lax.psum_scatter(
-            partial_value.astype(jnp.bfloat16), "row", scatter_dimension=0, tiled=True
-        ).astype(jnp.float32)
-        hidden = (
-            jax.nn.silu(summed[:, :hidden_width]) * summed[:, hidden_width:]
-        ).astype(jnp.bfloat16)
-        hidden = lax.all_gather(hidden, "row", axis=0, tiled=True)
+        gate_sums, up_sums = row_reduce_scatter(partial_value.astype(jnp.bfloat16), n_row)
+        hidden = (jax.nn.silu(gate_sums) * up_sums).astype(jnp.bfloat16)
+        hidden = row_all_gather(hidden, n_row)
         terms = jnp.dot(hidden, down_pruned, preferred_element_type=jnp.float32).astype(
             jnp.bfloat16
         )

time: 330 us -> 327 us (level)
  waiting for transfers between devices: 205 us -> 126 us
  blocking collectives: 0 us -> 56.3 us
  other arithmetic: 14.4 us -> 38.5 us
  matrix products: 45.2 us -> 30.6 us
  starting transfers between devices: 11.9 us -> 20.2 us
    ppermute x0 -> x14, waiting for transfers between devices: none -> 91.1 us  [the longest x6 54.6 us: row_reduce_scatter(): lax.ppermute(acc.astype(jnp.bfloat16), 'row', row_perm(n_row, direction))]
    unnamed x8 -> x1, waiting for transfers between devices: 73 us -> 0.71 us
    all_to_all x0 -> x1, blocking collectives: none -> 56.3 us  [on_device(): terms = lax.all_to_all(terms, 'col', 0, 0, tiled=False)]
    all_gather x2 -> x0, waiting for transfers between devices: 50.3 us -> none  [on_device(): hidden = lax.all_gather(hidden, 'row', axis=0, tiled=True)]
    all_to_all x2 -> x0, waiting for transfers between devices: 32.8 us -> none  [on_device(): terms = lax.all_to_all(terms, 'col', 0, 0, tiled=False)]
    unnamed x22 -> x18, local copies, waits for them, and re-layouts: 35.2 us -> 12 us
    ppermute x0 -> x14, starting transfers between devices: none -> 20.2 us  [the longest x6 10.2 us: row_all_gather(): held = lax.ppermute(held, 'row', row_perm(n_row, direction))]
    all_gather x2 -> x1, waiting for transfers between devices: 49 us -> 34.3 us  [on_device(): lax.all_gather(tokens[k * rows:(k + 1) * rows], 'col', axis=0, tiled=True)]
  transfers between devices with their start and end apart: 8 -> 15, of which waited for: 8 -> 10; matrix products, arithmetic and copies ran while one was open for 29% -> 11% of each run, Pallas kernels for 0% -> 0%
where the time goes in v2:
time: 327 us; the launch traced here: 326 us
  waiting for transfers between devices  126 us (39%)
  blocking collectives  56.3 us (17%)
  local copies, waits for them, and re-layouts  41 us (13%)
  other arithmetic  38.5 us (12%)
  matrix products  30.6 us (9%)
  starting transfers between devices  20.2 us (6%)
  between operations  13.7 us (4%)
    all_to_all x1, blocking collectives, on_device(): terms = lax.all_to_all(terms, 'col', 0, 0, tiled=False)  56.3 us
    ppermute x6, waiting for transfers between devices, row_reduce_scatter(): lax.ppermute(acc.astype(jnp.bfloat16), 'row', row_perm(n_row, direction))  54.6 us
    all_gather x1, waiting for transfers between devices, on_device(): lax.all_gather(tokens[k * rows:(k + 1) * rows], 'col', axis=0, tiled=True)  34.3 us
    dot_general x1, matrix products, on_device(): jnp.dot(chunk, both_weights, preferred_element_type=jnp.float32)  22.4 us
    ppermute x6, waiting for transfers between devices, row_all_gather(): held = lax.ppermute(held, 'row', row_perm(n_row, direction))  21.1 us
    add x1, other arithmetic, row_reduce_scatter(): keep.astype(jnp.float32)  12.5 us
    unnamed x18, local copies, waits for them, and re-layouts  12 us
    ppermute x1, waiting for transfers between devices, row_reduce_scatter(): lax.ppermute(send, 'row', swap).astype(jnp.float32)  12 us
  transfers between devices with their start and end apart: 15, of which 10 were waited for; matrix products, arithmetic and copies ran while one was open for 11% of the time, Pallas kernels for 0%

profile of v2, /device:TPU:0, one launch (start us, length us, event | category | flops | bytes accessed | tf_op | source)
XLA Modules:
  0.0 326.4 jit_solution(1611331296701454822)
XLA Ops:
  6.5 0.7 all-gather.2.cloned.1.call-update
  7.3 6.0 %copy.14 = bf16[1024,1792]{0,1:T(8,128)(2,1)} copy(bf16[1024,1792]{1,0:T(8,128)(2,1)} %param.12) | data formatting | bytes 7340032 | tf_op args[2]
  13.3 6.0 %copy.13 = bf16[1024,1792]{0,1:T(8,128)(2,1)} copy(bf16[1024,1792]{1,0:T(8,128)(2,1)} %param.11) | data formatting | bytes 7340032 | tf_op args[1]
  19.3 0.1 iota_compare_fusion.4
  19.4 0.3 fusion.17
  19.7 0.1 iota_compare_fusion.5
  19.8 0.3 fusion.15
  20.1 0.5 broadcast_in_dim.93
  20.7 5.1 %bitcast_select_fusion.1 = bf16[1024,1792]{0,1:T(8,128)(2,1)} fusion(bf16[1024,1792]{0,1:T(8,128)(2,1)} %copy.14, pred[224,8,8,128]{3,2,1,0:T(8,128)(4,1)S(1)} %bitcast.89), kind=kLoop, calls=%fused_computation.7 | loop fusion | flops 1835008 | bytes 9175040 | tf_op jit(solution)/shard_map/jit(_where)/select_n | solution.py:24
  25.8 0.5 broadcast_in_dim.90
  26.4 2.8 bitcast_select_fusion.2
  29.2 34.3 %all-gather.2.cloned.1.call-done = bf16[2048,1024]{1,0:T(8,128)(2,1)} async-done(((bf16[128,1024]{1,0:T(8,128)(2,1)}), bf16[2048,1024]{1,0:T(8,128)(2,1)}) %all-gather.2.cloned.1.call-update) | async-done | bytes 4194320 | tf_op jit(solution)/shard_map/all_gather | solution.py:114
  63.5 22.4 %convolution_convert_fusion = bf16[3584,2048]{0,1:T(8,128)(2,1)} fusion(bf16[2048,1024]{1,0:T(8,128)(2,1)} %all-gather.2.cloned.1.call-done, bf16[1024,1792]{0,1:T(8,128)(2,1)} %bitcast_select_fusion.1, bf16[1024,1792]{0,1:T(8,128)(2,1)} %bitcast_select_fusion.2), kind=kOutput, calls=%fused_computation | convolution fusion | flops 15054405632 | bytes 26214400 | tf_op jit(solution)/shard_map/dot_general | solution.py:115
  85.9 6.5 %dynamic-slice_bitcast_fusion = bf16[1024,3584]{1,0:T(8,128)(2,1)} fusion(bf16[2,1024,3584]{2,1,0:T(8,128)(2,1)} %bitcast.86, s32[]{:T(128)S(6)} %select_n.138), kind=kLoop, calls=%fused_computation.5 | loop fusion | bytes 14680068 | tf_op jit(solution)/shard_map/jit(dynamic_index_in_dim)/squeeze | solution.py:41
  92.3 12.0 %collective-permute-done = bf16[1024,3584]{1,0:T(8,128)(2,1)} collective-permute-done((bf16[1024,3584]{1,0:T(8,128)(2,1)}, bf16[1024,3584]{1,0:T(8,128)(2,1)}, u32[]{:S(2)}, u32[]{:S(2)}) %collective-permute-start) | collective-permute-done | bytes 7340064 | tf_op jit(solution)/shard_map/ppermute | solution.py:43
  104.3 12.5 %convert_add_fusion = f32[1024,3584]{1,0:T(8,128)} fusion(bf16[1024,3584]{1,0:T(8,128)(2,1)} %collective-permute-done, bf16[2,1024,3584]{2,1,0:T(8,128)(2,1)} %bitcast.87, s32[]{:T(128)S(6)} %select_n.137), kind=kLoop, calls=%fused_computation.1 | loop fusion | flops 11010048 | bytes 29360132 | tf_op jit(solution)/shard_map/add | solution.py:43
  116.8 11.5 %fusion.20 = (f32[4,256,1792]{2,1,0:T(8,128)}, f32[4,256,1792]{2,1,0:T(8,128)}) fusion(f32[4,256,3584]{2,1,0:T(8,128)} %bitcast.85), kind=kLoop, calls=%fused_computation.55 | loop fusion | bytes 29360128 | tf_op jit(solution)/shard_map/slice | solution.py:48
  128.3 1.6 fusion.10
  129.9 1.6 collective-permute-start.1
  131.4 1.6 fusion.11
  133.0 1.8 collective-permute-start.4
  134.8 18.7 %collective-permute-done.1 = bf16[256,1792]{1,0:T(8,128)(2,1)S(1)} collective-permute-done((bf16[256,1792]{1,0:T(8,128)(2,1)S(1)}, bf16[256,1792]{1,0:T(8,128)(2,1)S(1)}, u32[]{:S(2)}, u32[]{:S(2)}) %collective-permute-start.1) | collective-permute-done | bytes 917536 | tf_op jit(solution)/shard_map/ppermute | solution.py:52
  153.5 1.7 fusion.8
  155.2 0.3 collective-permute-start.2
  155.5 1.9 fusion.6
  157.4 3.0 collective-permute-start.5
  160.5 17.7 %collective-permute-done.2 = bf16[256,1792]{1,0:T(8,128)(2,1)} collective-permute-done((bf16[256,1792]{1,0:T(8,128)(2,1)S(1)}, bf16[256,1792]{1,0:T(8,128)(2,1)}, u32[]{:S(2)}, u32[]{:S(2)}) %collective-permute-start.2) | collective-permute-done | bytes 917536 | tf_op jit(solution)/shard_map/ppermute | solution.py:52
  178.1 1.9 fusion.7
  180.0 0.1 collective-permute-start.3
  180.1 2.8 fusion.5
  183.0 3.2 collective-permute-start.6
  186.2 15.8 %collective-permute-done.3 = bf16[256,1792]{1,0:T(8,128)(2,1)S(1)} collective-permute-done((bf16[256,1792]{1,0:T(8,128)(2,1)S(1)}, bf16[256,1792]{1,0:T(8,128)(2,1)S(1)}, u32[]{:S(2)}, u32[]{:S(2)}) %collective-permute-start.3) | collective-permute-done | bytes 917536 | tf_op jit(solution)/shard_map/ppermute | solution.py:52
  202.0 2.4 collective-permute-done.6
  204.4 2.7 fusion.4
  207.1 0.1 fusion.21
  207.2 0.1 collective-permute-start.7
  207.2 3.7 %collective-permute-start.10 = (bf16[256,896]{1,0:T(8,128)(2,1)S(1)}, bf16[256,896]{1,0:T(8,128)(2,1)S(1)}, u32[]{:S(2)}, u32[]{:S(2)}) collective-permute-start(bf16[256,896]{1,0:T(8,128)(2,1)S(1)} %get-tuple-element.8), channel_id=1, source_target_pairs={{0,96},{16,112},{32,0},{48,16},{64,32},{80,48},{96,64},{112,80},{1... | collective-permute-start | bytes 1376264 | tf_op jit(solution)/shard_map/ppermute | solution.py:71
  210.9 0.1 broadcast.73.clone.1
  211.0 0.1 bitcast_dynamic-update-slice_fusion.9
  211.1 0.1 broadcast.73.clone
  211.3 0.1 bitcast_dynamic-update-slice_fusion.5
  211.3 7.5 %collective-permute-done.7 = bf16[256,896]{1,0:T(8,128)(2,1)S(1)} collective-permute-done((bf16[256,896]{1,0:T(8,128)(2,1)S(1)}, bf16[256,896]{1,0:T(8,128)(2,1)S(1)}, u32[]{:S(2)}, u32[]{:S(2)}) %collective-permute-start.7) | collective-permute-done | bytes 458784 | tf_op jit(solution)/shard_map/ppermute | solution.py:71
  218.8 3.2 collective-permute-start.11
  222.1 0.1 bitcast_dynamic-update-slice_fusion.4
  222.1 7.3 %collective-permute-done.8 = bf16[256,896]{1,0:T(8,128)(2,1)S(1)} collective-permute-done((bf16[256,896]{1,0:T(8,128)(2,1)S(1)}, bf16[256,896]{1,0:T(8,128)(2,1)S(1)}, u32[]{:S(2)}, u32[]{:S(2)}) %collective-permute-start.8) | collective-permute-done | bytes 458784 | tf_op jit(solution)/shard_map/ppermute | solution.py:71
  229.5 3.2 collective-permute-start.12
  232.8 0.1 bitcast_dynamic-update-slice_fusion.3
  232.8 6.3 %collective-permute-done.9 = bf16[256,896]{1,0:T(8,128)(2,1)S(1)} collective-permute-done((bf16[256,896]{1,0:T(8,128)(2,1)S(1)}, bf16[256,896]{1,0:T(8,128)(2,1)S(1)}, u32[]{:S(2)}, u32[]{:S(2)}) %collective-permute-start.9) | collective-permute-done | bytes 458784 | tf_op jit(solution)/shard_map/ppermute | solution.py:71
  239.2 0.1 bitcast_dynamic-update-slice_fusion.2
  239.3 0.0 copy-start.6
  239.3 0.0 copy-start.1
  239.3 2.1 pad_maximum_fusion
  241.4 0.0 collective-permute-start.13
  241.4 0.1 iota_compare_fusion.3
  241.5 0.3 fusion.13
  241.8 0.5 broadcast_in_dim.89
  242.3 2.5 bitcast_dynamic-update-slice_fusion.1
  244.7 0.0 copy-start.7
  244.8 3.4 %collective-permute-done.13 = bf16[1024,1792]{1,0:T(8,128)(2,1)} collective-permute-done((bf16[1024,1792]{1,0:T(8,128)(2,1)}, bf16[1024,1792]{1,0:T(8,128)(2,1)}, u32[]{:S(2)}, u32[]{:S(2)}) %collective-permute-start.13) | collective-permute-done | bytes 3670048 | tf_op jit(solution)/shard_map/ppermute | solution.py:76
  248.1 2.5 bitcast_dynamic-update-slice_fusion
  250.6 0.5 broadcast_in_dim.105
  251.2 8.2 %convolution_convert_fusion.1 = bf16[2048,1024]{1,0:T(8,128)(2,1)S(1)} fusion(bf16[2048,1792]{1,0:T(8,128)(2,1)S(1)} %bitcast.88, bf16[1792,1024]{1,0:T(8,128)(2,1)S(1)} %copy-done.7, pred[224,8,8,128]{3,2,1,0:T(8,128)(4,1)S(1)} %bitcast.92), kind=kOutput, calls=%fused_computation.9 | convolution fusion | flops 7520124928 | bytes 17039360 | tf_op jit(solution)/shard_map/dot_general | solution.py:119
  259.4 56.3 %all_to_all.5 = bf16[16,128,1024]{2,1,0:T(8,128)(2,1)} all-to-all(bf16[16,128,1024]{2,1,0:T(8,128)(2,1)S(1)} %bitcast.91), channel_id=1, replica_groups=mesh['row'=8,'col'=16] {'col'}, dimensions={0} | all-to-all | bytes 8388608 | tf_op jit(solution)/shard_map/all_to_all | solution.py:124
  315.7 3.9 %reduce_sum.12 = bf16[128,1024]{1,0:T(8,128)(2,1)} reduce(bf16[16,128,1024]{2,1,0:T(8,128)(2,1)} %all_to_all.5, bf16[]{:T(256)} %constant.162.clone.1), dimensions={0}, to_apply=%region_3.4 | reduce | flops 1966080 | bytes 4456450 | tf_op jit(solution)/shard_map/reduce_sum | solution.py:125
  (27 shorter events, 0.2 us)
Async XLA Ops:
  6.5 57.0 %all-gather.2.cloned.1.call-start = ((), (), s32[]{:S(2)}) async-start(), calls=%async_computation.1 | async-start | bytes 4456448 | tf_op jit(solution)/shard_map/all_gather | solution.py:114
  13.3 6.0 %copy-start.4 = (s32[14]{0:T(128)S(1)}, s32[14]{0:T(128)}, u32[]{:S(2)}) copy-start(s32[14]{0:T(128)} %param.17) | copy-start | bytes 172
  13.3 6.1 %copy-start.2 = (s32[14,48]{1,0:T(8,128)S(1)}, s32[14,48]{1,0:T(8,128)}, u32[]{:S(2)}) copy-start(s32[14,48]{1,0:T(8,128)} %param.16) | copy-start | bytes 8068
  13.3 6.1 %copy-start.3 = (s32[14,48]{1,0:T(8,128)S(1)}, s32[14,48]{1,0:T(8,128)}, u32[]{:S(2)}) copy-start(s32[14,48]{1,0:T(8,128)} %param.14) | copy-start | bytes 8068
  13.3 6.5 %copy-start.5 = (s32[14]{0:T(128)S(1)}, s32[14]{0:T(128)}, u32[]{:S(2)}) copy-start(s32[14]{0:T(128)} %param.15) | copy-start | bytes 172
  20.7 5.7 %copy-start = (bf16[1024,1792]{0,1:T(8,128)(2,1)S(1)}, bf16[1024,1792]{0,1:T(8,128)(2,1)}, u32[]{:S(2)}) copy-start(bf16[1024,1792]{0,1:T(8,128)(2,1)} %copy.13) | copy-start | bytes 11010052
  92.3 12.0 %collective-permute-start = (bf16[1024,3584]{1,0:T(8,128)(2,1)}, bf16[1024,3584]{1,0:T(8,128)(2,1)}, u32[]{:S(2)}, u32[]{:S(2)}) collective-permute-start(bf16[1024,3584]{1,0:T(8,128)(2,1)} %dynamic-slice_bitcast_fusion), channel_id=1, source_target_pairs={{0,16},{16,0},{32,48},{48,32},{64,80},{80,64},{96,112},{112,96},{1... | collective-permute-start | bytes 22020104 | tf_op jit(solution)/shard_map/ppermute | solution.py:43
  129.9 23.7 %collective-permute-start.1 = (bf16[256,1792]{1,0:T(8,128)(2,1)S(1)}, bf16[256,1792]{1,0:T(8,128)(2,1)S(1)}, u32[]{:S(2)}, u32[]{:S(2)}) collective-permute-start(bf16[256,1792]{1,0:T(8,128)(2,1)S(1)} %fusion.10), channel_id=1, source_target_pairs={{0,32},{16,48},{32,64},{48,80},{64,96},{80,112},{96,0},{112,16},{1... | collective-permute-start | bytes 2752520 | tf_op jit(solution)/shard_map/ppermute | solution.py:52
  133.0 22.5 %collective-permute-start.4 = (bf16[256,1792]{1,0:T(8,128)(2,1)S(1)}, bf16[256,1792]{1,0:T(8,128)(2,1)}, u32[]{:S(2)}, u32[]{:S(2)}) collective-permute-start(bf16[256,1792]{1,0:T(8,128)(2,1)S(1)} %fusion.11), channel_id=1, source_target_pairs={{0,96},{16,112},{32,0},{48,16},{64,32},{80,48},{96,64},{112,80},{1... | collective-permute-start | bytes 2752520 | tf_op jit(solution)/shard_map/ppermute | solution.py:52
  155.2 22.9 %collective-permute-start.2 = (bf16[256,1792]{1,0:T(8,128)(2,1)S(1)}, bf16[256,1792]{1,0:T(8,128)(2,1)}, u32[]{:S(2)}, u32[]{:S(2)}) collective-permute-start(bf16[256,1792]{1,0:T(8,128)(2,1)S(1)} %fusion.8), channel_id=1, source_target_pairs={{0,32},{16,48},{32,64},{48,80},{64,96},{80,112},{96,0},{112,16},{1... | collective-permute-start | bytes 2752520 | tf_op jit(solution)/shard_map/ppermute | solution.py:52
  157.4 22.7 %collective-permute-start.5 = (bf16[256,1792]{1,0:T(8,128)(2,1)S(1)}, bf16[256,1792]{1,0:T(8,128)(2,1)}, u32[]{:S(2)}, u32[]{:S(2)}) collective-permute-start(bf16[256,1792]{1,0:T(8,128)(2,1)S(1)} %fusion.6), channel_id=1, source_target_pairs={{0,96},{16,112},{32,0},{48,16},{64,32},{80,48},{96,64},{112,80},{1... | collective-permute-start | bytes 2752520 | tf_op jit(solution)/shard_map/ppermute | solution.py:52
  180.0 22.0 %collective-permute-start.3 = (bf16[256,1792]{1,0:T(8,128)(2,1)S(1)}, bf16[256,1792]{1,0:T(8,128)(2,1)S(1)}, u32[]{:S(2)}, u32[]{:S(2)}) collective-permute-start(bf16[256,1792]{1,0:T(8,128)(2,1)S(1)} %fusion.7), channel_id=1, source_target_pairs={{0,32},{16,48},{32,64},{48,80},{64,96},{80,112},{96,0},{112,16},{1... | collective-permute-start | bytes 2752520 | tf_op jit(solution)/shard_map/ppermute | solution.py:52
  183.0 21.4 %collective-permute-start.6 = (bf16[256,1792]{1,0:T(8,128)(2,1)}, bf16[256,1792]{1,0:T(8,128)(2,1)S(1)}, u32[]{:S(2)}, u32[]{:S(2)}) collective-permute-start(bf16[256,1792]{1,0:T(8,128)(2,1)} %fusion.5), channel_id=1, source_target_pairs={{0,96},{16,112},{32,0},{48,16},{64,32},{80,48},{96,64},{112,80},{1... | collective-permute-start | bytes 2752520 | tf_op jit(solution)/shard_map/ppermute | solution.py:52
  207.2 11.6 %collective-permute-start.7 = (bf16[256,896]{1,0:T(8,128)(2,1)S(1)}, bf16[256,896]{1,0:T(8,128)(2,1)S(1)}, u32[]{:S(2)}, u32[]{:S(2)}) collective-permute-start(bf16[256,896]{1,0:T(8,128)(2,1)S(1)} %get-tuple-element.7), channel_id=1, source_target_pairs={{0,32},{16,48},{32,64},{48,80},{64,96},{80,112},{96,0},{112,16},{1... | collective-permute-start | bytes 1376264 | tf_op jit(solution)/shard_map/ppermute | solution.py:71
  207.2 11.6 %collective-permute-start.10 = (bf16[256,896]{1,0:T(8,128)(2,1)S(1)}, bf16[256,896]{1,0:T(8,128)(2,1)S(1)}, u32[]{:S(2)}, u32[]{:S(2)}) collective-permute-start(bf16[256,896]{1,0:T(8,128)(2,1)S(1)} %get-tuple-element.8), channel_id=1, source_target_pairs={{0,96},{16,112},{32,0},{48,16},{64,32},{80,48},{96,64},{112,80},{1... | collective-permute-start | bytes 1376264 | tf_op jit(solution)/shard_map/ppermute | solution.py:71
  218.8 10.7 %collective-permute-start.8 = (bf16[256,896]{1,0:T(8,128)(2,1)S(1)}, bf16[256,896]{1,0:T(8,128)(2,1)S(1)}, u32[]{:S(2)}, u32[]{:S(2)}) collective-permute-start(bf16[256,896]{1,0:T(8,128)(2,1)S(1)} %collective-permute-done.7), channel_id=1, source_target_pairs={{0,32},{16,48},{32,64},{48,80},{64,96},{80,112},{96,0},{112,16},{1... | collective-permute-start | bytes 1376264 | tf_op jit(solution)/shard_map/ppermute | solution.py:71
  218.8 10.7 %collective-permute-start.11 = (bf16[256,896]{1,0:T(8,128)(2,1)S(1)}, bf16[256,896]{1,0:T(8,128)(2,1)S(1)}, u32[]{:S(2)}, u32[]{:S(2)}) collective-permute-start(bf16[256,896]{1,0:T(8,128)(2,1)S(1)} %collective-permute-done.10), channel_id=1, source_target_pairs={{0,96},{16,112},{32,0},{48,16},{64,32},{80,48},{96,64},{112,80},{1... | collective-permute-start | bytes 1376264 | tf_op jit(solution)/shard_map/ppermute | solution.py:71
  229.5 9.7 %collective-permute-start.9 = (bf16[256,896]{1,0:T(8,128)(2,1)S(1)}, bf16[256,896]{1,0:T(8,128)(2,1)S(1)}, u32[]{:S(2)}, u32[]{:S(2)}) collective-permute-start(bf16[256,896]{1,0:T(8,128)(2,1)S(1)} %collective-permute-done.8), channel_id=1, source_target_pairs={{0,32},{16,48},{32,64},{48,80},{64,96},{80,112},{96,0},{112,16},{1... | collective-permute-start | bytes 1376264 | tf_op jit(solution)/shard_map/ppermute | solution.py:71
  229.5 9.7 %collective-permute-start.12 = (bf16[256,896]{1,0:T(8,128)(2,1)S(1)}, bf16[256,896]{1,0:T(8,128)(2,1)S(1)}, u32[]{:S(2)}, u32[]{:S(2)}) collective-permute-start(bf16[256,896]{1,0:T(8,128)(2,1)S(1)} %collective-permute-done.11), channel_id=1, source_target_pairs={{0,96},{16,112},{32,0},{48,16},{64,32},{80,48},{96,64},{112,80},{1... | collective-permute-start | bytes 1376264 | tf_op jit(solution)/shard_map/ppermute | solution.py:71
  239.3 2.1 copy-start.6
  239.3 2.2 copy-start.1
  241.4 6.8 %collective-permute-start.13 = (bf16[1024,1792]{1,0:T(8,128)(2,1)}, bf16[1024,1792]{1,0:T(8,128)(2,1)}, u32[]{:S(2)}, u32[]{:S(2)}) collective-permute-start(bf16[1024,1792]{1,0:T(8,128)(2,1)} %bitcast.25), channel_id=1, source_target_pairs={{0,16},{16,0},{32,48},{48,32},{64,80},{80,64},{96,112},{112,96},{1... | collective-permute-start | bytes 11010056 | tf_op jit(solution)/shard_map/ppermute | solution.py:76
  244.7 6.4 %copy-start.7 = (bf16[1792,1024]{1,0:T(8,128)(2,1)S(1)}, bf16[1792,1024]{1,0:T(8,128)(2,1)}, u32[]{:S(2)}) copy-start(bf16[1792,1024]{1,0:T(8,128)(2,1)} %param.13) | copy-start | bytes 11010052
Sparse Core Ops, SparseCore 0:
  9.5 53.9 all-gather.1
